TPU v7x, 32 devices: a whole 2x2x4 slice. The times are simulated.
32 devices in a mesh: area: 16 (over z, y, core), depth: 2 (over x).
Axes of the slice: x: 2, y: 2, z: 4, core: 2. Of those that a mesh axis runs over, the one named last changes fastest.
Arguments:
- pressure: float32 [32, 128, 1024], P('depth', 'area'), may hold values from -2.5 to -0.3
- theta_old: float32 [32, 128, 1024], P('depth', 'area'), may hold values from 0.1 to 0.35
- source: float32 [32, 128, 1024], P('depth', 'area'), may hold values from -3 to 3
- soil_type: int32 [32, 128, 1024], P('depth', 'area'), may hold values from 0 to 11
- soil_params: float32 [5, 12], replicated, as said below
Outputs:
- new_pressure: float32 [32, 128, 1024], P('depth', 'area')
- coarse_head: float32 [128, 1024], P('area')
Inputs may be any that keep to these rules, and one draw needn't show every extreme that they name: Each column of soil_params holds theta_r in 0.03 to 0.1, theta_s in 0.35 to 0.5, a in 0.5 to 3, n in 1.3 to 2.5, Ks in 0.2 to 2.
All inputs are finite; a program needn't handle non-finite values.
Results may differ from a plain program's by a relative error of at most 0.00002.
Values sent between devices are 32-bit elements; how exact they have to be, the bound alone decides.
No kernel may reach another device: no remote copies, remote signals or barrier semaphores. Data moves between devices by JAX's collectives and lax.ppermute only.
A program may use at most 64 MiB of HBM per device.

v0:
```python
import jax
import jax.numpy as jnp
from jax import lax
from jax.sharding import PartitionSpec as P

step_time = 0.1
relax = 0.8
small_suction = 0.04


def with_halo(block, sides, width):
    for axis, dim in sides:
        count = lax.axis_size(axis)
        forward = [(i, i + 1) for i in range(count - 1)]
        backward = [(target, source) for source, target in forward]
        low = lax.ppermute(
            lax.slice_in_dim(block, block.shape[dim] - width, None, axis=dim), axis, forward
        )
        high = lax.ppermute(lax.slice_in_dim(block, 0, width, axis=dim), axis, backward)
        block = jnp.concatenate([low, block, high], axis=dim)
    return block


def soil_fields(soil_type, soil_params):
    fields = []
    for row_id in range(5):
        picked = jnp.zeros(soil_type.shape, jnp.float32)
        for kind_id in range(soil_params.shape[1]):
            picked = jnp.where(soil_type == kind_id, soil_params[row_id, kind_id], picked)
        fields.append(picked)
    return fields


def hydraulics(pressure, params):
    theta_r, theta_s, alpha_vg, shape_n, k_sat = params
    suction = jnp.sqrt(pressure * pressure + small_suction)
    shape_m = 1.0 - 1.0 / shape_n
    power_term = jnp.exp(shape_n * jnp.log(alpha_vg * suction))
    one_plus = 1.0 + power_term
    saturation = jnp.exp(-shape_m * jnp.log(one_plus))
    content = theta_r + (theta_s - theta_r) * saturation
    capacity = (
        (theta_s - theta_r) * shape_m * shape_n * power_term * saturation / (one_plus * suction)
    )
    ratio_term = power_term / one_plus
    conduct = (
        k_sat * jnp.sqrt(saturation) * jnp.square(1.0 - jnp.exp(shape_m * jnp.log(ratio_term)))
    )
    return (content, capacity, conduct)


def fine_balance(padded_head, padded_cond, content, capacity, theta_old, source):
    centre_h = padded_head[1:-1, 1:-1, 1:-1]
    centre_k = padded_cond[1:-1, 1:-1, 1:-1]
    inflow = jnp.zeros_like(centre_h)
    totals = jnp.zeros_like(centre_h)
    for axis_pos in range(3):
        for offset, weight in ((0, 1.0), (2, -1.0)):
            window = [slice(1, -1)] * 3
            window[axis_pos] = slice(offset, offset + centre_h.shape[axis_pos])
            near_h = padded_head[tuple(window)]
            near_k = padded_cond[tuple(window)]
            face_k = jnp.sqrt(centre_k * near_k)
            inflow = inflow + face_k * (near_h - centre_h)
            totals = totals + face_k
            if axis_pos == 0:
                inflow = inflow + weight * face_k
    balance = (content - theta_old) / step_time - inflow - source
    diagonal = capacity / step_time + totals
    return (balance, diagonal)


def coarse_balance(padded_head, padded_trans, storage, base):
    centre_h = padded_head[1:-1, 1:-1]
    centre_t = padded_trans[1:-1, 1:-1]
    inflow = jnp.zeros_like(centre_h)
    totals = jnp.zeros_like(centre_h)
    for axis_pos in range(2):
        for offset in (0, 2):
            window = [slice(1, -1)] * 2
            window[axis_pos] = slice(offset, offset + centre_h.shape[axis_pos])
            face_t = jnp.sqrt(centre_t * padded_trans[tuple(window)])
            inflow = inflow + face_t * (padded_head[tuple(window)] - centre_h)
            totals = totals + face_t
    balance = storage / step_time * (centre_h - base) - inflow
    diagonal = storage / step_time + totals
    return (balance, diagonal)


def coarse_rim_rows(stacked):
    extended = with_halo(stacked, (("area", 1),), 1)
    return jnp.pad(extended, ((0, 0), (0, 0), (1, 1)))


def coarse_cycle(columns, depth_total, rim_rows):
    column_kh = columns[0]
    column_k = columns[1]
    storage = columns[2]
    restricted = columns[3]
    column_rate = columns[4] / depth_total
    base = column_kh / column_k
    padded = rim_rows(jnp.stack([base, column_k]))
    start_flow, start_diag = coarse_balance(padded[0], padded[1], storage, base)
    coarse_rhs = start_flow + restricted
    first = base - relax * (start_flow - coarse_rhs) / start_diag
    transmit = column_k * jnp.exp(column_rate * jnp.tanh(first - base))
    padded = rim_rows(jnp.stack([first, transmit]))
    first_flow, first_diag = coarse_balance(padded[0], padded[1], storage, base)
    second = first - relax * (first_flow - coarse_rhs) / first_diag
    return (base, second)


def shards(pressure, theta_old, source, soil_type, soil_params):
    depth_total = pressure.shape[0] * lax.axis_size("depth")
    params = soil_fields(soil_type, soil_params)
    content, capacity, conduct = hydraulics(pressure, params)
    extended = with_halo(jnp.stack([pressure, conduct]), (("area", 2), ("depth", 1)), 1)
    extended = jnp.pad(extended, ((0, 0), (0, 0), (0, 0), (1, 1)))
    balance, diagonal = fine_balance(extended[0], extended[1], content, capacity, theta_old, source)
    smoothed = pressure - relax * balance / diagonal
    content, capacity, conduct = hydraulics(smoothed, params)
    extended = with_halo(jnp.stack([smoothed, conduct]), (("area", 2), ("depth", 1)), 1)
    extended = jnp.pad(extended, ((0, 0), (0, 0), (0, 0), (1, 1)))
    balance, diagonal = fine_balance(extended[0], extended[1], content, capacity, theta_old, source)
    local_sums = jnp.stack(
        [
            jnp.sum(conduct * smoothed, axis=0),
            jnp.sum(conduct, axis=0),
            jnp.sum(capacity, axis=0),
            -jnp.sum(balance, axis=0),
            jnp.sum(params[2], axis=0),
        ]
    )
    columns = lax.psum(local_sums, "depth")
    base, second = coarse_cycle(columns, depth_total, coarse_rim_rows)
    return (smoothed + (second - base)[None], second)


def solution(mesh):
    in_specs = (
        P("depth", "area", None),
        P("depth", "area", None),
        P("depth", "area", None),
        P("depth", "area", None),
        P(),
    )
    out_specs = (P("depth", "area", None), P("area", None))
    return jax.shard_map(shards, mesh=mesh, in_specs=in_specs, out_specs=out_specs, check_vma=False)
```

profile of v0, /device:TPU:5, one launch (start us, length us, event | category | flops | bytes accessed | tf_op | source)
XLA Modules:
  0.0 171.1 jit_solution(90720884499490197)
XLA Ops:
  7.2 2.1 %fusion.109 = (f32[1,1]{1,0:T(1,128)}, f32[1,1]{1,0:T(1,128)}, f32[1,1]{1,0:T(1,128)}, f32[1,1]{1,0:T(1,128)}, f32[1,1]{1,0:T(1,128)}, /*index=5*/f32[1,1]{1,0:T...) fusion(f32[5,12]{1,0:T(8,128)} %param.9), kind=kLoop, calls=%fused_computation.233 | loop fusion | bytes 152 | tf_op jit(solution)/shard_map/slice | solution.py:29
  9.3 2.1 %fusion.108 = (f32[1,1]{1,0:T(1,128)}, f32[1,1]{1,0:T(1,128)}, f32[1,1]{1,0:T(1,128)}, f32[1,1]{1,0:T(1,128)}, f32[1,1]{1,0:T(1,128)}, /*index=5*/f32[1,1]{1,0:T...) fusion(f32[5,12]{1,0:T(8,128)} %param.9), kind=kLoop, calls=%fused_computation.232 | loop fusion | bytes 152 | tf_op jit(solution)/shard_map/slice | solution.py:29
  12.8 9.6 %fusion.105 = (f32[8,1024]{1,0:T(8,128)S(1)}, f32[16,8,1024]{2,1,0:T(8,128)S(1)}, pred[16,8,1024]{2,1,0:T(8,128)(4,1)S(1)}, pred[16,8,1024]{2,1,0:T(8,128)(4,1)S...) fusion(f32[]{:T(128)} %bitcast.47, f32[]{:T(128)} %bitcast.46, ...), kind=kLoop, calls=%fused_computation.231 | loop fusion | flops 3268608 | bytes 2654256 | tf_op jit(solution)/shard_map/reduce_sum | solution.py:131
  22.5 16.5 %fusion.63 = (f32[1,16,8,1024]{3,2,1,0:T(8,128)S(1)}, f32[16,8,1024]{2,1,0:T(8,128)S(1)}, f32[16,8,1024]{2,1,0:T(8,128)S(1)}) fusion(f32[16,8,1024]{2,1,0:T(8,128)S(1)} %get-tuple-element.11, f32[16,8,1024]{2,1,0:T(8,128)S(1)} %copy-done, pred[16,8,1024]{2,1,0:T(8,128)(4,1)S(1)} %get-tuple-element.23, pred[16,8,1024]{2,1,0:T(8,128)(4,1)S(1)} %get-tuple-element.22, ...), kind=kLoop, calls=%fused_computation.123 | loop fusion | flops 5111808 | bytes 4194400 | tf_op jit(solution)/shard_map/stack | solution.py:117
  39.1 3.7 %collective-permute-start = (f32[2,16,1,1024]{3,2,1,0:T(1,128)S(1)}, f32[2,16,1,1024]{3,2,1,0:T(1,128)S(1)}, u32[]{:S(2)}, u32[]{:S(2)}) collective-permute-start(f32[2,16,1,1024]{3,2,1,0:T(1,128)S(1)} %get-tuple-element.41), channel_id=1, source_target_pairs={{0,2},{2,4},{4,6},{6,8},{8,10},{10,12},{12,14},{14,16},{16,18},{18... | collective-permute-start | bytes 393224 | tf_op jit(solution)/shard_map/ppermute | solution.py:16
  42.8 1.9 %collective-permute-start.1 = (f32[2,16,1,1024]{3,2,1,0:T(1,128)S(1)}, f32[2,16,1,1024]{3,2,1,0:T(1,128)S(1)}, u32[]{:S(2)}, u32[]{:S(2)}) collective-permute-start(f32[2,16,1,1024]{3,2,1,0:T(1,128)S(1)} %get-tuple-element.42), channel_id=1, source_target_pairs={{2,0},{4,2},{6,4},{8,6},{10,8},{12,10},{14,12},{16,14},{18,16},{20... | collective-permute-start | bytes 393224 | tf_op jit(solution)/shard_map/ppermute | solution.py:19
  44.8 5.2 %collective-permute-done.1 = f32[2,16,1,1024]{3,2,1,0:T(1,128)S(1)} collective-permute-done((f32[2,16,1,1024]{3,2,1,0:T(1,128)S(1)}, f32[2,16,1,1024]{3,2,1,0:T(1,128)S(1)}, u32[]{:S(2)}, u32[]{:S(2)}) %collective-permute-start.1) | collective-permute-done | bytes 131104 | tf_op jit(solution)/shard_map/ppermute | solution.py:19
  50.1 3.1 %collective-permute-start.2 = (f32[2,1,10,1024]{3,2,1,0:T(8,128)S(1)}, f32[2,1,10,1024]{3,2,1,0:T(8,128)S(1)}, u32[]{:S(2)}, u32[]{:S(2)}) collective-permute-start(f32[2,1,10,1024]{3,2,1,0:T(8,128)S(1)} %get-tuple-element.37), channel_id=1, source_target_pairs={{0,1},{2,3},{4,5},{6,7},{8,9},{10,11},{12,13},{14,15},{16,17},{18,... | collective-permute-start | bytes 245768 | tf_op jit(solution)/shard_map/ppermute | solution.py:16
  55.3 3.7 %collective-permute-done.3 = f32[2,1,10,1024]{3,2,1,0:T(8,128)S(1)} collective-permute-done((f32[2,1,10,1024]{3,2,1,0:T(8,128)S(1)}, f32[2,1,10,1024]{3,2,1,0:T(8,128)S(1)}, u32[]{:S(2)}, u32[]{:S(2)}) %collective-permute-start.3) | collective-permute-done | bytes 81952 | tf_op jit(solution)/shard_map/ppermute | solution.py:19
  58.9 1.5 select_maximum_fusion.5
  61.7 19.8 %fusion.62 = (f32[8,1024]{1,0:T(8,128)S(1)}, f32[16,8,1024]{2,1,0:T(8,128)S(1)}, f32[16,8,1024]{2,1,0:T(8,128)S(1)}) fusion(f32[16,8,1024]{2,1,0:T(8,128)S(1)} %get-tuple-element.29, pred[16,8,1024]{2,1,0:T(8,128)(4,1)S(1)} %get-tuple-element.23, pred[16,8,1024]{2,1,0:T(8,128)(4,1)S(1)} %get-tuple-element.22, ...), kind=kLoop, calls=%fused_computation.122 | loop fusion | flops 12181504 | bytes 12615776 | tf_op jit(solution)/shard_map/reduce_sum | solution.py:129
  82.3 4.2 %collective-permute-start.4 = (f32[2,16,1,1024]{3,2,1,0:T(1,128)S(1)}, f32[2,16,1,1024]{3,2,1,0:T(1,128)S(1)}, u32[]{:S(2)}, u32[]{:S(2)}) collective-permute-start(f32[2,16,1,1024]{3,2,1,0:T(1,128)S(1)} %get-tuple-element.39), channel_id=1, source_target_pairs={{0,2},{2,4},{4,6},{6,8},{8,10},{10,12},{12,14},{14,16},{16,18},{18... | collective-permute-start | bytes 393224 | tf_op jit(solution)/shard_map/ppermute | solution.py:16
  86.5 1.9 %collective-permute-start.5 = (f32[2,16,1,1024]{3,2,1,0:T(1,128)S(1)}, f32[2,16,1,1024]{3,2,1,0:T(1,128)S(1)}, u32[]{:S(2)}, u32[]{:S(2)}) collective-permute-start(f32[2,16,1,1024]{3,2,1,0:T(1,128)S(1)} %get-tuple-element.40), channel_id=1, source_target_pairs={{2,0},{4,2},{6,4},{8,6},{10,8},{12,10},{14,12},{16,14},{18,16},{20... | collective-permute-start | bytes 393224 | tf_op jit(solution)/shard_map/ppermute | solution.py:19
  88.5 5.2 %collective-permute-done.5 = f32[2,16,1,1024]{3,2,1,0:T(1,128)S(1)} collective-permute-done((f32[2,16,1,1024]{3,2,1,0:T(1,128)S(1)}, f32[2,16,1,1024]{3,2,1,0:T(1,128)S(1)}, u32[]{:S(2)}, u32[]{:S(2)}) %collective-permute-start.5) | collective-permute-done | bytes 131104 | tf_op jit(solution)/shard_map/ppermute | solution.py:19
  97.0 3.8 %collective-permute-done.7 = f32[2,1,10,1024]{3,2,1,0:T(8,128)S(1)} collective-permute-done((f32[2,1,10,1024]{3,2,1,0:T(8,128)S(1)}, f32[2,1,10,1024]{3,2,1,0:T(8,128)S(1)}, u32[]{:S(2)}, u32[]{:S(2)}) %collective-permute-start.7) | collective-permute-done | bytes 81952 | tf_op jit(solution)/shard_map/ppermute | solution.py:19
  100.8 1.5 select_maximum_fusion
  102.5 18.4 %fusion.64 = f32[8,1024]{1,0:T(8,128)S(1)} fusion(f32[16,8,1024]{2,1,0:T(8,128)S(1)} %copy-done.1, f32[18,10,1026]{2,1,0:T(8,128)S(1)} %get-tuple-element.32, f32[18,10,1026]{2,1,0:T(8,128)S(1)} %get-tuple-element.31, f32[16,8,1024]{2,1,0:T(8,128)S(1)} %copy-done.2, f32[16,8,1024]{2,1,0:T(8,128)S(1)} %get-tuple-element.25, ...), kind=kLoop, calls=%fused_computation.124 | loop fusion | flops 8249344 | bytes 11042912 | tf_op jit(solution)/shard_map/reduce_sum | solution.py:130
  121.6 20.4 %all-reduce.6.cloned.1.call-done = f32[5,8,1024]{2,1,0:T(8,128)} async-done(((f32[5,8,1024]{2,1,0:T(8,128)}), f32[5,8,1024]{2,1,0:T(8,128)}) %all-reduce.6.cloned.1.call-update) | async-done | bytes 163856 | tf_op jit(solution)/shard_map/psum | solution.py:134
  142.8 4.1 %collective-permute-start.8 = (f32[2,1,1024]{2,1,0:T(1,128)S(1)}, f32[2,1,1024]{2,1,0:T(1,128)S(1)}, u32[]{:S(2)}, u32[]{:S(2)}) collective-permute-start(f32[2,1,1024]{2,1,0:T(1,128)S(1)} %get-tuple-element.51), channel_id=1, source_target_pairs={{0,2},{2,4},{4,6},{6,8},{8,10},{10,12},{12,14},{14,16},{16,18},{18... | collective-permute-start | bytes 24584 | tf_op jit(solution)/shard_map/ppermute | solution.py:16
  146.9 1.9 %collective-permute-start.9 = (f32[2,1,1024]{2,1,0:T(1,128)S(1)}, f32[2,1,1024]{2,1,0:T(1,128)S(1)}, u32[]{:S(2)}, u32[]{:S(2)}) collective-permute-start(f32[2,1,1024]{2,1,0:T(1,128)S(1)} %get-tuple-element.52), channel_id=1, source_target_pairs={{2,0},{4,2},{6,4},{8,6},{10,8},{12,10},{14,12},{16,14},{18,16},{20... | collective-permute-start | bytes 24584 | tf_op jit(solution)/shard_map/ppermute | solution.py:19
  148.8 3.9 %collective-permute-done.9 = f32[2,1,1024]{2,1,0:T(1,128)S(1)} collective-permute-done((f32[2,1,1024]{2,1,0:T(1,128)S(1)}, f32[2,1,1024]{2,1,0:T(1,128)S(1)}, u32[]{:S(2)}, u32[]{:S(2)}) %collective-permute-start.9) | collective-permute-done | bytes 8224 | tf_op jit(solution)/shard_map/ppermute | solution.py:19
  153.9 1.9 %collective-permute-start.10 = (f32[2,1,1024]{2,1,0:T(1,128)S(1)}, f32[2,1,1024]{2,1,0:T(1,128)S(1)}, u32[]{:S(2)}, u32[]{:S(2)}) collective-permute-start(f32[2,1,1024]{2,1,0:T(1,128)S(1)} %get-tuple-element.49), channel_id=1, source_target_pairs={{0,2},{2,4},{4,6},{6,8},{8,10},{10,12},{12,14},{14,16},{16,18},{18... | collective-permute-start | bytes 24584 | tf_op jit(solution)/shard_map/ppermute | solution.py:16
  155.9 2.4 %collective-permute-start.11 = (f32[2,1,1024]{2,1,0:T(1,128)S(1)}, f32[2,1,1024]{2,1,0:T(1,128)S(1)}, u32[]{:S(2)}, u32[]{:S(2)}) collective-permute-start(f32[2,1,1024]{2,1,0:T(1,128)S(1)} %get-tuple-element.50), channel_id=1, source_target_pairs={{2,0},{4,2},{6,4},{8,6},{10,8},{12,10},{14,12},{16,14},{18,16},{20... | collective-permute-start | bytes 24584 | tf_op jit(solution)/shard_map/ppermute | solution.py:19
  158.3 3.5 %collective-permute-done.11 = f32[2,1,1024]{2,1,0:T(1,128)S(1)} collective-permute-done((f32[2,1,1024]{2,1,0:T(1,128)S(1)}, f32[2,1,1024]{2,1,0:T(1,128)S(1)}, u32[]{:S(2)}, u32[]{:S(2)}) %collective-permute-start.11) | collective-permute-done | bytes 8224 | tf_op jit(solution)/shard_map/ppermute | solution.py:19
  (45 shorter events, 14.2 us)
Async XLA Ops:
  7.2 15.3 %copy-start = (f32[16,8,1024]{2,1,0:T(8,128)S(1)}, f32[16,8,1024]{2,1,0:T(8,128)}, u32[]{:S(2)}) copy-start(f32[16,8,1024]{2,1,0:T(8,128)} %param.5) | copy-start | bytes 1572868
  7.2 134.8 %all-reduce.6.cloned.1.call-start = ((), (), s32[]{:S(2)}) async-start(), calls=%async_computation | async-start | bytes 327680 | tf_op jit(solution)/shard_map/psum | solution.py:134
  22.5 32.0 %copy-start.4 = (f32[5,12]{1,0:T(8,128)S(1)}, f32[5,12]{1,0:T(8,128)}, u32[]{:S(2)}) copy-start(f32[5,12]{1,0:T(8,128)} %param.9) | copy-start | bytes 724
  39.1 5.6 %collective-permute-start = (f32[2,16,1,1024]{3,2,1,0:T(1,128)S(1)}, f32[2,16,1,1024]{3,2,1,0:T(1,128)S(1)}, u32[]{:S(2)}, u32[]{:S(2)}) collective-permute-start(f32[2,16,1,1024]{3,2,1,0:T(1,128)S(1)} %get-tuple-element.41), channel_id=1, source_target_pairs={{0,2},{2,4},{4,6},{6,8},{8,10},{10,12},{12,14},{14,16},{16,18},{18... | collective-permute-start | bytes 393224 | tf_op jit(solution)/shard_map/ppermute | solution.py:16
  42.8 7.2 %collective-permute-start.1 = (f32[2,16,1,1024]{3,2,1,0:T(1,128)S(1)}, f32[2,16,1,1024]{3,2,1,0:T(1,128)S(1)}, u32[]{:S(2)}, u32[]{:S(2)}) collective-permute-start(f32[2,16,1,1024]{3,2,1,0:T(1,128)S(1)} %get-tuple-element.42), channel_id=1, source_target_pairs={{2,0},{4,2},{6,4},{8,6},{10,8},{12,10},{14,12},{16,14},{18,16},{20... | collective-permute-start | bytes 393224 | tf_op jit(solution)/shard_map/ppermute | solution.py:19
  50.1 5.2 %collective-permute-start.2 = (f32[2,1,10,1024]{3,2,1,0:T(8,128)S(1)}, f32[2,1,10,1024]{3,2,1,0:T(8,128)S(1)}, u32[]{:S(2)}, u32[]{:S(2)}) collective-permute-start(f32[2,1,10,1024]{3,2,1,0:T(8,128)S(1)} %get-tuple-element.37), channel_id=1, source_target_pairs={{0,1},{2,3},{4,5},{6,7},{8,9},{10,11},{12,13},{14,15},{16,17},{18,... | collective-permute-start | bytes 245768 | tf_op jit(solution)/shard_map/ppermute | solution.py:16
  53.2 5.7 %collective-permute-start.3 = (f32[2,1,10,1024]{3,2,1,0:T(8,128)S(1)}, f32[2,1,10,1024]{3,2,1,0:T(8,128)S(1)}, u32[]{:S(2)}, u32[]{:S(2)}) collective-permute-start(f32[2,1,10,1024]{3,2,1,0:T(8,128)S(1)} %get-tuple-element.38), channel_id=1, source_target_pairs={{1,0},{3,2},{5,4},{7,6},{9,8},{11,10},{13,12},{15,14},{17,16},{19,... | collective-permute-start | bytes 245768 | tf_op jit(solution)/shard_map/ppermute | solution.py:19
  60.5 1.0 copy-start.1
  60.5 1.2 copy-start.2
  82.3 6.2 %collective-permute-start.4 = (f32[2,16,1,1024]{3,2,1,0:T(1,128)S(1)}, f32[2,16,1,1024]{3,2,1,0:T(1,128)S(1)}, u32[]{:S(2)}, u32[]{:S(2)}) collective-permute-start(f32[2,16,1,1024]{3,2,1,0:T(1,128)S(1)} %get-tuple-element.39), channel_id=1, source_target_pairs={{0,2},{2,4},{4,6},{6,8},{8,10},{10,12},{12,14},{14,16},{16,18},{18... | collective-permute-start | bytes 393224 | tf_op jit(solution)/shard_map/ppermute | solution.py:16
  86.5 7.2 %collective-permute-start.5 = (f32[2,16,1,1024]{3,2,1,0:T(1,128)S(1)}, f32[2,16,1,1024]{3,2,1,0:T(1,128)S(1)}, u32[]{:S(2)}, u32[]{:S(2)}) collective-permute-start(f32[2,16,1,1024]{3,2,1,0:T(1,128)S(1)} %get-tuple-element.40), channel_id=1, source_target_pairs={{2,0},{4,2},{6,4},{8,6},{10,8},{12,10},{14,12},{16,14},{18,16},{20... | collective-permute-start | bytes 393224 | tf_op jit(solution)/shard_map/ppermute | solution.py:19
  93.7 3.2 %collective-permute-start.6 = (f32[2,1,10,1024]{3,2,1,0:T(8,128)S(1)}, f32[2,1,10,1024]{3,2,1,0:T(8,128)S(1)}, u32[]{:S(2)}, u32[]{:S(2)}) collective-permute-start(f32[2,1,10,1024]{3,2,1,0:T(8,128)S(1)} %get-tuple-element.35), channel_id=1, source_target_pairs={{0,1},{2,3},{4,5},{6,7},{8,9},{10,11},{12,13},{14,15},{16,17},{18,... | collective-permute-start | bytes 245768 | tf_op jit(solution)/shard_map/ppermute | solution.py:16
  95.1 5.7 %collective-permute-start.7 = (f32[2,1,10,1024]{3,2,1,0:T(8,128)S(1)}, f32[2,1,10,1024]{3,2,1,0:T(8,128)S(1)}, u32[]{:S(2)}, u32[]{:S(2)}) collective-permute-start(f32[2,1,10,1024]{3,2,1,0:T(8,128)S(1)} %get-tuple-element.36), channel_id=1, source_target_pairs={{1,0},{3,2},{5,4},{7,6},{9,8},{11,10},{13,12},{15,14},{17,16},{19,... | collective-permute-start | bytes 245768 | tf_op jit(solution)/shard_map/ppermute | solution.py:19
  120.9 0.7 copy-start.3
  142.8 6.0 %collective-permute-start.8 = (f32[2,1,1024]{2,1,0:T(1,128)S(1)}, f32[2,1,1024]{2,1,0:T(1,128)S(1)}, u32[]{:S(2)}, u32[]{:S(2)}) collective-permute-start(f32[2,1,1024]{2,1,0:T(1,128)S(1)} %get-tuple-element.51), channel_id=1, source_target_pairs={{0,2},{2,4},{4,6},{6,8},{8,10},{10,12},{12,14},{14,16},{16,18},{18... | collective-permute-start | bytes 24584 | tf_op jit(solution)/shard_map/ppermute | solution.py:16
  146.9 5.9 %collective-permute-start.9 = (f32[2,1,1024]{2,1,0:T(1,128)S(1)}, f32[2,1,1024]{2,1,0:T(1,128)S(1)}, u32[]{:S(2)}, u32[]{:S(2)}) collective-permute-start(f32[2,1,1024]{2,1,0:T(1,128)S(1)} %get-tuple-element.52), channel_id=1, source_target_pairs={{2,0},{4,2},{6,4},{8,6},{10,8},{12,10},{14,12},{16,14},{18,16},{20... | collective-permute-start | bytes 24584 | tf_op jit(solution)/shard_map/ppermute | solution.py:19
  153.9 4.3 %collective-permute-start.10 = (f32[2,1,1024]{2,1,0:T(1,128)S(1)}, f32[2,1,1024]{2,1,0:T(1,128)S(1)}, u32[]{:S(2)}, u32[]{:S(2)}) collective-permute-start(f32[2,1,1024]{2,1,0:T(1,128)S(1)} %get-tuple-element.49), channel_id=1, source_target_pairs={{0,2},{2,4},{4,6},{6,8},{8,10},{10,12},{12,14},{14,16},{16,18},{18... | collective-permute-start | bytes 24584 | tf_op jit(solution)/shard_map/ppermute | solution.py:16
  155.9 5.9 %collective-permute-start.11 = (f32[2,1,1024]{2,1,0:T(1,128)S(1)}, f32[2,1,1024]{2,1,0:T(1,128)S(1)}, u32[]{:S(2)}, u32[]{:S(2)}) collective-permute-start(f32[2,1,1024]{2,1,0:T(1,128)S(1)} %get-tuple-element.50), channel_id=1, source_target_pairs={{2,0},{4,2},{6,4},{8,6},{10,8},{12,10},{14,12},{16,14},{18,16},{20... | collective-permute-start | bytes 24584 | tf_op jit(solution)/shard_map/ppermute | solution.py:19
Sparse Core Ops, SparseCore 0:
  121.7 20.1 all-reduce.5
where the time goes:
time: 173 us; the launch traced here: 171 us
  other arithmetic  72.9 us (42%)
  waiting for transfers between devices  46.1 us (27%)
  starting transfers between devices  29.4 us (17%)
  between operations  14.4 us (8%)
  local copies, waits for them, and re-layouts  8.38 us (5%)
    ppermute x6, waiting for transfers between devices, with_halo(): lax.ppermute(lax.slice_in_dim(block, 0, width, axis=dim), axis, backward)  25.3 us
    psum x1, waiting for transfers between devices, shards(): columns = lax.psum(local_sums, 'depth')  20.4 us
    reduce_sum x1, other arithmetic, shards(): jnp.sum(capacity, axis=0)  19.8 us
    ppermute x6, starting transfers between devices, with_halo(): lax.ppermute(lax.slice_in_dim(block, block.shape[dim] - width, None, axis...  18.4 us
    reduce_sum x1, other arithmetic, shards(): jnp.sum(balance, axis=0)  18.4 us
    another operation x1, other arithmetic, shards(): jnp.stack([pressure, conduct])  16.5 us
    ppermute x6, starting transfers between devices, with_halo(): lax.ppermute(lax.slice_in_dim(block, 0, width, axis=dim), axis, backward)  10.9 us
    reduce_sum x1, other arithmetic, shards(): jnp.sum(params[2], axis=0)  9.63 us
  transfers between devices with their start and end apart: 13, of which 8 were waited for; matrix products, arithmetic and copies ran while one was open for 0% of the time, Pallas kernels for 0%

commit v1 on v0

--- a/solution.py
+++ b/solution.py
@@ -131,7 +131,7 @@
             jnp.sum(params[2], axis=0),
         ]
     )
-    columns = lax.psum(local_sums, "depth")
+    columns = jnp.sum(lax.all_gather(local_sums, "depth"), axis=0)
     base, second = coarse_cycle(columns, depth_total, coarse_rim_rows)
     return (smoothed + (second - base)[None], second)
 

time: 173 us -> 141 us (0.82)
  waiting for transfers between devices: 46.1 us -> 25.8 us
  between operations: 14.4 us -> 1 us
  blocking collectives: 0 us -> 4.85 us
  other arithmetic: 72.9 us -> 70.7 us
    psum x1 -> x0, waiting for transfers between devices: 20.4 us -> none  [shards(): columns = lax.psum(local_sums, 'depth')]
    all_gather x0 -> x1, blocking collectives: none -> 4.85 us  [shards(): columns = jnp.sum(lax.all_gather(local_sums, 'depth'), axis=0)]
  transfers between devices with their start and end apart: 13 -> 12, of which waited for: 8 -> 7; matrix products, arithmetic and copies ran while one was open for 0% -> 1% of each run, Pallas kernels for 0% -> 0%
where the time goes in v1:
time: 141 us; the launch traced here: 139 us
  other arithmetic  70.7 us (50%)
  starting transfers between devices  29.4 us (21%)
  waiting for transfers between devices  25.8 us (18%)
  local copies, waits for them, and re-layouts  7.75 us (5%)
  blocking collectives  4.85 us (3%)
    ppermute x6, waiting for transfers between devices, with_halo(): lax.ppermute(lax.slice_in_dim(block, 0, width, axis=dim), axis, backward)  25.3 us
    reduce_sum x1, other arithmetic, shards(): jnp.sum(capacity, axis=0)  19.9 us
    ppermute x6, starting transfers between devices, with_halo(): lax.ppermute(lax.slice_in_dim(block, block.shape[dim] - width, None, axis...  18.5 us
    reduce_sum x1, other arithmetic, shards(): jnp.sum(balance, axis=0)  18.4 us
    another operation x1, other arithmetic, shards(): jnp.stack([pressure, conduct])  16.5 us
    ppermute x6, starting transfers between devices, with_halo(): lax.ppermute(lax.slice_in_dim(block, 0, width, axis=dim), axis, backward)  10.9 us
    reduce_sum x1, other arithmetic, shards(): jnp.sum(params[2], axis=0)  9.67 us
    slice x4, local copies, waits for them, and re-layouts, soil_fields(): soil_params[row_id, kind_id]  6.34 us
  transfers between devices with their start and end apart: 12, of which 7 were waited for; matrix products, arithmetic and copies ran while one was open for 1% of the time, Pallas kernels for 0%

profile of v1, /device:TPU:5, one launch (start us, length us, event | category | flops | bytes accessed | tf_op | source)
XLA Modules:
  0.0 139.5 jit_solution(2432604296362628139)
XLA Ops:
  0.6 2.1 %fusion.109 = (f32[1,1]{1,0:T(1,128)}, f32[1,1]{1,0:T(1,128)}, f32[1,1]{1,0:T(1,128)}, f32[1,1]{1,0:T(1,128)}, f32[1,1]{1,0:T(1,128)}, /*index=5*/f32[1,1]{1,0:T...) fusion(f32[5,12]{1,0:T(8,128)} %param.9), kind=kLoop, calls=%fused_computation.233 | loop fusion | bytes 152 | tf_op jit(solution)/shard_map/slice | solution.py:29
  2.7 2.1 %fusion.108 = (f32[1,1]{1,0:T(1,128)}, f32[1,1]{1,0:T(1,128)}, f32[1,1]{1,0:T(1,128)}, f32[1,1]{1,0:T(1,128)}, f32[1,1]{1,0:T(1,128)}, /*index=5*/f32[1,1]{1,0:T...) fusion(f32[5,12]{1,0:T(8,128)} %param.9), kind=kLoop, calls=%fused_computation.232 | loop fusion | bytes 152 | tf_op jit(solution)/shard_map/slice | solution.py:29
  6.3 9.7 %fusion.105 = (f32[8,1024]{1,0:T(8,128)S(1)}, f32[16,8,1024]{2,1,0:T(8,128)S(1)}, pred[16,8,1024]{2,1,0:T(8,128)(4,1)S(1)}, pred[16,8,1024]{2,1,0:T(8,128)(4,1)S...) fusion(f32[]{:T(128)} %bitcast.47, f32[]{:T(128)} %bitcast.46, ...), kind=kLoop, calls=%fused_computation.231 | loop fusion | flops 3268608 | bytes 2654256 | tf_op jit(solution)/shard_map/reduce_sum | solution.py:131
  16.0 16.5 %fusion.63 = (f32[1,16,8,1024]{3,2,1,0:T(8,128)S(1)}, f32[16,8,1024]{2,1,0:T(8,128)S(1)}, f32[16,8,1024]{2,1,0:T(8,128)S(1)}) fusion(f32[16,8,1024]{2,1,0:T(8,128)S(1)} %get-tuple-element.11, f32[16,8,1024]{2,1,0:T(8,128)S(1)} %copy-done, pred[16,8,1024]{2,1,0:T(8,128)(4,1)S(1)} %get-tuple-element.23, pred[16,8,1024]{2,1,0:T(8,128)(4,1)S(1)} %get-tuple-element.22, ...), kind=kLoop, calls=%fused_computation.123 | loop fusion | flops 5111808 | bytes 4194400 | tf_op jit(solution)/shard_map/stack | solution.py:117
  32.7 3.7 %collective-permute-start = (f32[2,16,1,1024]{3,2,1,0:T(1,128)S(1)}, f32[2,16,1,1024]{3,2,1,0:T(1,128)S(1)}, u32[]{:S(2)}, u32[]{:S(2)}) collective-permute-start(f32[2,16,1,1024]{3,2,1,0:T(1,128)S(1)} %get-tuple-element.41), channel_id=1, source_target_pairs={{0,2},{2,4},{4,6},{6,8},{8,10},{10,12},{12,14},{14,16},{16,18},{18... | collective-permute-start | bytes 393224 | tf_op jit(solution)/shard_map/ppermute | solution.py:16
  36.4 1.9 %collective-permute-start.1 = (f32[2,16,1,1024]{3,2,1,0:T(1,128)S(1)}, f32[2,16,1,1024]{3,2,1,0:T(1,128)S(1)}, u32[]{:S(2)}, u32[]{:S(2)}) collective-permute-start(f32[2,16,1,1024]{3,2,1,0:T(1,128)S(1)} %get-tuple-element.42), channel_id=1, source_target_pairs={{2,0},{4,2},{6,4},{8,6},{10,8},{12,10},{14,12},{16,14},{18,16},{20... | collective-permute-start | bytes 393224 | tf_op jit(solution)/shard_map/ppermute | solution.py:19
  38.3 5.2 %collective-permute-done.1 = f32[2,16,1,1024]{3,2,1,0:T(1,128)S(1)} collective-permute-done((f32[2,16,1,1024]{3,2,1,0:T(1,128)S(1)}, f32[2,16,1,1024]{3,2,1,0:T(1,128)S(1)}, u32[]{:S(2)}, u32[]{:S(2)}) %collective-permute-start.1) | collective-permute-done | bytes 131104 | tf_op jit(solution)/shard_map/ppermute | solution.py:19
  43.6 3.1 %collective-permute-start.2 = (f32[2,1,10,1024]{3,2,1,0:T(8,128)S(1)}, f32[2,1,10,1024]{3,2,1,0:T(8,128)S(1)}, u32[]{:S(2)}, u32[]{:S(2)}) collective-permute-start(f32[2,1,10,1024]{3,2,1,0:T(8,128)S(1)} %get-tuple-element.37), channel_id=1, source_target_pairs={{0,1},{2,3},{4,5},{6,7},{8,9},{10,11},{12,13},{14,15},{16,17},{18,... | collective-permute-start | bytes 245768 | tf_op jit(solution)/shard_map/ppermute | solution.py:16
  48.8 3.7 %collective-permute-done.3 = f32[2,1,10,1024]{3,2,1,0:T(8,128)S(1)} collective-permute-done((f32[2,1,10,1024]{3,2,1,0:T(8,128)S(1)}, f32[2,1,10,1024]{3,2,1,0:T(8,128)S(1)}, u32[]{:S(2)}, u32[]{:S(2)}) %collective-permute-start.3) | collective-permute-done | bytes 81952 | tf_op jit(solution)/shard_map/ppermute | solution.py:19
  52.5 1.6 %select_maximum_fusion.5 = f32[2,18,10,1026]{3,2,1,0:T(8,128)S(1)} fusion(f32[2,1,10,1024]{3,2,1,0:T(8,128)S(1)} %collective-permute-done.3, f32[2,1,10,1024]{3,2,1,0:T(8,128)S(1)} %collective-permute-done.2, f32[2,16,1,1024]{3,2,1,0:T(1,128)S(1)} %collective-permute-done.1, f32[2,16,1,1024]{3,2,1,0:T(1,128)S(1)} %collective-permute-done, ...), kind=kLoop, calls=%fused_computation.7 | loop fusion | flops 5171040 | bytes 2952000 | tf_op jit(solution)/shard_map/concatenate | solution.py:20
  55.2 19.9 %fusion.62 = (f32[8,1024]{1,0:T(8,128)S(1)}, f32[16,8,1024]{2,1,0:T(8,128)S(1)}, f32[16,8,1024]{2,1,0:T(8,128)S(1)}) fusion(f32[16,8,1024]{2,1,0:T(8,128)S(1)} %get-tuple-element.29, pred[16,8,1024]{2,1,0:T(8,128)(4,1)S(1)} %get-tuple-element.23, pred[16,8,1024]{2,1,0:T(8,128)(4,1)S(1)} %get-tuple-element.22, ...), kind=kLoop, calls=%fused_computation.122 | loop fusion | flops 12181504 | bytes 12615776 | tf_op jit(solution)/shard_map/reduce_sum | solution.py:129
  75.8 4.2 %collective-permute-start.4 = (f32[2,16,1,1024]{3,2,1,0:T(1,128)S(1)}, f32[2,16,1,1024]{3,2,1,0:T(1,128)S(1)}, u32[]{:S(2)}, u32[]{:S(2)}) collective-permute-start(f32[2,16,1,1024]{3,2,1,0:T(1,128)S(1)} %get-tuple-element.39), channel_id=1, source_target_pairs={{0,2},{2,4},{4,6},{6,8},{8,10},{10,12},{12,14},{14,16},{16,18},{18... | collective-permute-start | bytes 393224 | tf_op jit(solution)/shard_map/ppermute | solution.py:16
  80.1 1.9 %collective-permute-start.5 = (f32[2,16,1,1024]{3,2,1,0:T(1,128)S(1)}, f32[2,16,1,1024]{3,2,1,0:T(1,128)S(1)}, u32[]{:S(2)}, u32[]{:S(2)}) collective-permute-start(f32[2,16,1,1024]{3,2,1,0:T(1,128)S(1)} %get-tuple-element.40), channel_id=1, source_target_pairs={{2,0},{4,2},{6,4},{8,6},{10,8},{12,10},{14,12},{16,14},{18,16},{20... | collective-permute-start | bytes 393224 | tf_op jit(solution)/shard_map/ppermute | solution.py:19
  82.0 5.2 %collective-permute-done.5 = f32[2,16,1,1024]{3,2,1,0:T(1,128)S(1)} collective-permute-done((f32[2,16,1,1024]{3,2,1,0:T(1,128)S(1)}, f32[2,16,1,1024]{3,2,1,0:T(1,128)S(1)}, u32[]{:S(2)}, u32[]{:S(2)}) %collective-permute-start.5) | collective-permute-done | bytes 131104 | tf_op jit(solution)/shard_map/ppermute | solution.py:19
  90.6 3.8 %collective-permute-done.7 = f32[2,1,10,1024]{3,2,1,0:T(8,128)S(1)} collective-permute-done((f32[2,1,10,1024]{3,2,1,0:T(8,128)S(1)}, f32[2,1,10,1024]{3,2,1,0:T(8,128)S(1)}, u32[]{:S(2)}, u32[]{:S(2)}) %collective-permute-start.7) | collective-permute-done | bytes 81952 | tf_op jit(solution)/shard_map/ppermute | solution.py:19
  94.3 1.5 %select_maximum_fusion = f32[2,18,10,1026]{3,2,1,0:T(8,128)S(1)} fusion(f32[2,1,10,1024]{3,2,1,0:T(8,128)S(1)} %collective-permute-done.7, f32[2,1,10,1024]{3,2,1,0:T(8,128)S(1)} %collective-permute-done.6, f32[2,16,1,1024]{3,2,1,0:T(1,128)S(1)} %collective-permute-done.5, f32[2,16,1,1024]{3,2,1,0:T(1,128)S(1)} %collective-permute-done.4, ...), kind=kLoop, calls=%fused_computation.2 | loop fusion | flops 5171040 | bytes 2952000 | tf_op jit(solution)/shard_map/concatenate | solution.py:20
  96.1 18.4 %fusion.64 = f32[8,1024]{1,0:T(8,128)S(1)} fusion(f32[16,8,1024]{2,1,0:T(8,128)S(1)} %copy-done.1, f32[18,10,1026]{2,1,0:T(8,128)S(1)} %get-tuple-element.32, f32[18,10,1026]{2,1,0:T(8,128)S(1)} %get-tuple-element.31, f32[16,8,1024]{2,1,0:T(8,128)S(1)} %copy-done.2, f32[16,8,1024]{2,1,0:T(8,128)S(1)} %get-tuple-element.25, ...), kind=kLoop, calls=%fused_computation.124 | loop fusion | flops 8249344 | bytes 11042912 | tf_op jit(solution)/shard_map/reduce_sum | solution.py:130
  114.5 4.8 %all-gather = f32[10,8,1024]{2,1,0:T(8,128)S(1)} all-gather(f32[5,8,1024]{2,1,0:T(8,128)S(1)} %bitcast_dynamic-update-slice_fusion), channel_id=2, replica_groups=mesh['area'=16,'depth'=2] {'depth'}, dimensions={0}, use_global_device_ids=true | all-gather | bytes 491520 | tf_op jit(solution)/shard_map/all_gather | solution.py:134
  119.4 4.2 %collective-permute-start.8 = (f32[2,1,1024]{2,1,0:T(1,128)S(1)}, f32[2,1,1024]{2,1,0:T(1,128)S(1)}, u32[]{:S(2)}, u32[]{:S(2)}) collective-permute-start(f32[2,1,1024]{2,1,0:T(1,128)S(1)} %get-tuple-element.51), channel_id=1, source_target_pairs={{0,2},{2,4},{4,6},{6,8},{8,10},{10,12},{12,14},{14,16},{16,18},{18... | collective-permute-start | bytes 24584 | tf_op jit(solution)/shard_map/ppermute | solution.py:16
  123.7 1.9 %collective-permute-start.9 = (f32[2,1,1024]{2,1,0:T(1,128)S(1)}, f32[2,1,1024]{2,1,0:T(1,128)S(1)}, u32[]{:S(2)}, u32[]{:S(2)}) collective-permute-start(f32[2,1,1024]{2,1,0:T(1,128)S(1)} %get-tuple-element.52), channel_id=1, source_target_pairs={{2,0},{4,2},{6,4},{8,6},{10,8},{12,10},{14,12},{16,14},{18,16},{20... | collective-permute-start | bytes 24584 | tf_op jit(solution)/shard_map/ppermute | solution.py:19
  125.6 3.9 %collective-permute-done.9 = f32[2,1,1024]{2,1,0:T(1,128)S(1)} collective-permute-done((f32[2,1,1024]{2,1,0:T(1,128)S(1)}, f32[2,1,1024]{2,1,0:T(1,128)S(1)}, u32[]{:S(2)}, u32[]{:S(2)}) %collective-permute-start.9) | collective-permute-done | bytes 8224 | tf_op jit(solution)/shard_map/ppermute | solution.py:19
  129.9 1.9 %collective-permute-start.10 = (f32[2,1,1024]{2,1,0:T(1,128)S(1)}, f32[2,1,1024]{2,1,0:T(1,128)S(1)}, u32[]{:S(2)}, u32[]{:S(2)}) collective-permute-start(f32[2,1,1024]{2,1,0:T(1,128)S(1)} %get-tuple-element.49), channel_id=1, source_target_pairs={{0,2},{2,4},{4,6},{6,8},{8,10},{10,12},{12,14},{14,16},{16,18},{18... | collective-permute-start | bytes 24584 | tf_op jit(solution)/shard_map/ppermute | solution.py:16
  131.9 2.4 %collective-permute-start.11 = (f32[2,1,1024]{2,1,0:T(1,128)S(1)}, f32[2,1,1024]{2,1,0:T(1,128)S(1)}, u32[]{:S(2)}, u32[]{:S(2)}) collective-permute-start(f32[2,1,1024]{2,1,0:T(1,128)S(1)} %get-tuple-element.50), channel_id=1, source_target_pairs={{2,0},{4,2},{6,4},{8,6},{10,8},{12,10},{14,12},{16,14},{18,16},{20... | collective-permute-start | bytes 24584 | tf_op jit(solution)/shard_map/ppermute | solution.py:19
  134.3 3.5 %collective-permute-done.11 = f32[2,1,1024]{2,1,0:T(1,128)S(1)} collective-permute-done((f32[2,1,1024]{2,1,0:T(1,128)S(1)}, f32[2,1,1024]{2,1,0:T(1,128)S(1)}, u32[]{:S(2)}, u32[]{:S(2)}) %collective-permute-start.11) | collective-permute-done | bytes 8224 | tf_op jit(solution)/shard_map/ppermute | solution.py:19
  (42 shorter events, 11.2 us)
Async XLA Ops:
  0.6 15.3 %copy-start = (f32[16,8,1024]{2,1,0:T(8,128)S(1)}, f32[16,8,1024]{2,1,0:T(8,128)}, u32[]{:S(2)}) copy-start(f32[16,8,1024]{2,1,0:T(8,128)} %param.5) | copy-start | bytes 1572868
  15.9 32.1 %copy-start.3 = (f32[5,12]{1,0:T(8,128)S(1)}, f32[5,12]{1,0:T(8,128)}, u32[]{:S(2)}) copy-start(f32[5,12]{1,0:T(8,128)} %param.9) | copy-start | bytes 724
  32.7 5.6 %collective-permute-start = (f32[2,16,1,1024]{3,2,1,0:T(1,128)S(1)}, f32[2,16,1,1024]{3,2,1,0:T(1,128)S(1)}, u32[]{:S(2)}, u32[]{:S(2)}) collective-permute-start(f32[2,16,1,1024]{3,2,1,0:T(1,128)S(1)} %get-tuple-element.41), channel_id=1, source_target_pairs={{0,2},{2,4},{4,6},{6,8},{8,10},{10,12},{12,14},{14,16},{16,18},{18... | collective-permute-start | bytes 393224 | tf_op jit(solution)/shard_map/ppermute | solution.py:16
  36.4 7.2 %collective-permute-start.1 = (f32[2,16,1,1024]{3,2,1,0:T(1,128)S(1)}, f32[2,16,1,1024]{3,2,1,0:T(1,128)S(1)}, u32[]{:S(2)}, u32[]{:S(2)}) collective-permute-start(f32[2,16,1,1024]{3,2,1,0:T(1,128)S(1)} %get-tuple-element.42), channel_id=1, source_target_pairs={{2,0},{4,2},{6,4},{8,6},{10,8},{12,10},{14,12},{16,14},{18,16},{20... | collective-permute-start | bytes 393224 | tf_op jit(solution)/shard_map/ppermute | solution.py:19
  43.6 5.2 %collective-permute-start.2 = (f32[2,1,10,1024]{3,2,1,0:T(8,128)S(1)}, f32[2,1,10,1024]{3,2,1,0:T(8,128)S(1)}, u32[]{:S(2)}, u32[]{:S(2)}) collective-permute-start(f32[2,1,10,1024]{3,2,1,0:T(8,128)S(1)} %get-tuple-element.37), channel_id=1, source_target_pairs={{0,1},{2,3},{4,5},{6,7},{8,9},{10,11},{12,13},{14,15},{16,17},{18,... | collective-permute-start | bytes 245768 | tf_op jit(solution)/shard_map/ppermute | solution.py:16
  46.7 5.7 %collective-permute-start.3 = (f32[2,1,10,1024]{3,2,1,0:T(8,128)S(1)}, f32[2,1,10,1024]{3,2,1,0:T(8,128)S(1)}, u32[]{:S(2)}, u32[]{:S(2)}) collective-permute-start(f32[2,1,10,1024]{3,2,1,0:T(8,128)S(1)} %get-tuple-element.38), channel_id=1, source_target_pairs={{1,0},{3,2},{5,4},{7,6},{9,8},{11,10},{13,12},{15,14},{17,16},{19,... | collective-permute-start | bytes 245768 | tf_op jit(solution)/shard_map/ppermute | solution.py:19
  54.0 1.0 copy-start.1
  54.0 1.2 copy-start.2
  75.8 6.2 %collective-permute-start.4 = (f32[2,16,1,1024]{3,2,1,0:T(1,128)S(1)}, f32[2,16,1,1024]{3,2,1,0:T(1,128)S(1)}, u32[]{:S(2)}, u32[]{:S(2)}) collective-permute-start(f32[2,16,1,1024]{3,2,1,0:T(1,128)S(1)} %get-tuple-element.39), channel_id=1, source_target_pairs={{0,2},{2,4},{4,6},{6,8},{8,10},{10,12},{12,14},{14,16},{16,18},{18... | collective-permute-start | bytes 393224 | tf_op jit(solution)/shard_map/ppermute | solution.py:16
  80.1 7.2 %collective-permute-start.5 = (f32[2,16,1,1024]{3,2,1,0:T(1,128)S(1)}, f32[2,16,1,1024]{3,2,1,0:T(1,128)S(1)}, u32[]{:S(2)}, u32[]{:S(2)}) collective-permute-start(f32[2,16,1,1024]{3,2,1,0:T(1,128)S(1)} %get-tuple-element.40), channel_id=1, source_target_pairs={{2,0},{4,2},{6,4},{8,6},{10,8},{12,10},{14,12},{16,14},{18,16},{20... | collective-permute-start | bytes 393224 | tf_op jit(solution)/shard_map/ppermute | solution.py:19
  87.3 3.2 %collective-permute-start.6 = (f32[2,1,10,1024]{3,2,1,0:T(8,128)S(1)}, f32[2,1,10,1024]{3,2,1,0:T(8,128)S(1)}, u32[]{:S(2)}, u32[]{:S(2)}) collective-permute-start(f32[2,1,10,1024]{3,2,1,0:T(8,128)S(1)} %get-tuple-element.35), channel_id=1, source_target_pairs={{0,1},{2,3},{4,5},{6,7},{8,9},{10,11},{12,13},{14,15},{16,17},{18,... | collective-permute-start | bytes 245768 | tf_op jit(solution)/shard_map/ppermute | solution.py:16
  88.6 5.7 %collective-permute-start.7 = (f32[2,1,10,1024]{3,2,1,0:T(8,128)S(1)}, f32[2,1,10,1024]{3,2,1,0:T(8,128)S(1)}, u32[]{:S(2)}, u32[]{:S(2)}) collective-permute-start(f32[2,1,10,1024]{3,2,1,0:T(8,128)S(1)} %get-tuple-element.36), channel_id=1, source_target_pairs={{1,0},{3,2},{5,4},{7,6},{9,8},{11,10},{13,12},{15,14},{17,16},{19,... | collective-permute-start | bytes 245768 | tf_op jit(solution)/shard_map/ppermute | solution.py:19
  119.4 6.2 %collective-permute-start.8 = (f32[2,1,1024]{2,1,0:T(1,128)S(1)}, f32[2,1,1024]{2,1,0:T(1,128)S(1)}, u32[]{:S(2)}, u32[]{:S(2)}) collective-permute-start(f32[2,1,1024]{2,1,0:T(1,128)S(1)} %get-tuple-element.51), channel_id=1, source_target_pairs={{0,2},{2,4},{4,6},{6,8},{8,10},{10,12},{12,14},{14,16},{16,18},{18... | collective-permute-start | bytes 24584 | tf_op jit(solution)/shard_map/ppermute | solution.py:16
  123.7 5.9 %collective-permute-start.9 = (f32[2,1,1024]{2,1,0:T(1,128)S(1)}, f32[2,1,1024]{2,1,0:T(1,128)S(1)}, u32[]{:S(2)}, u32[]{:S(2)}) collective-permute-start(f32[2,1,1024]{2,1,0:T(1,128)S(1)} %get-tuple-element.52), channel_id=1, source_target_pairs={{2,0},{4,2},{6,4},{8,6},{10,8},{12,10},{14,12},{16,14},{18,16},{20... | collective-permute-start | bytes 24584 | tf_op jit(solution)/shard_map/ppermute | solution.py:19
  129.9 4.3 %collective-permute-start.10 = (f32[2,1,1024]{2,1,0:T(1,128)S(1)}, f32[2,1,1024]{2,1,0:T(1,128)S(1)}, u32[]{:S(2)}, u32[]{:S(2)}) collective-permute-start(f32[2,1,1024]{2,1,0:T(1,128)S(1)} %get-tuple-element.49), channel_id=1, source_target_pairs={{0,2},{2,4},{4,6},{6,8},{8,10},{10,12},{12,14},{14,16},{16,18},{18... | collective-permute-start | bytes 24584 | tf_op jit(solution)/shard_map/ppermute | solution.py:16
  131.9 5.9 %collective-permute-start.11 = (f32[2,1,1024]{2,1,0:T(1,128)S(1)}, f32[2,1,1024]{2,1,0:T(1,128)S(1)}, u32[]{:S(2)}, u32[]{:S(2)}) collective-permute-start(f32[2,1,1024]{2,1,0:T(1,128)S(1)} %get-tuple-element.50), channel_id=1, source_target_pairs={{2,0},{4,2},{6,4},{8,6},{10,8},{12,10},{14,12},{16,14},{18,16},{20... | collective-permute-start | bytes 24584 | tf_op jit(solution)/shard_map/ppermute | solution.py:19
